TPU v7x, 128 devices: a whole 4x4x4 slice. The times are simulated.
128 devices in a mesh: frames: 2 (over core), pix: 64 (over z, y, x).
Axes of the slice: x: 4, y: 4, z: 4, core: 2. Of those that a mesh axis runs over, the one named last changes fastest.
Arguments:
- frames: float32 [256, 32768], P('frames', 'pix'), may hold values from -6 to 6
Outputs:
- sketch: float32 [128, 32768], P(None, 'pix')
- projected: float32 [256, 32768], P('frames', 'pix')
All inputs are finite; a program needn't handle non-finite values.
Results may differ from a plain program's by a relative error of at most 0.0003.
Values sent between devices are 32-bit elements; how exact they have to be, the bound alone decides.
A program may use at most 64 MiB of HBM per device.

v0:
```python
import jax
import jax.numpy as jnp
from jax import lax
from jax.sharding import PartitionSpec as P


def in_blocks(array, dim, size):
    before, after = (array.shape[:dim], array.shape[dim + 1 :])
    return jnp.moveaxis(array.reshape(*before, size, -1, *after), dim, 0)


def summed_on_arrival(array, axis, dim):
    size = lax.axis_size(axis)
    pieces = lax.all_to_all(in_blocks(array, dim, size), axis, 0, 0, tiled=True)
    return jnp.sum(pieces, axis=0)


def rows_for(lines, size):
    spare = -lines.shape[0] % size
    if not spare:
        return lines
    return jnp.concatenate([lines, jnp.zeros((spare, *lines.shape[1:]), lines.dtype)])


def laid_out(pieces, dim):
    pieces = jnp.moveaxis(pieces, 0, dim)
    shape = pieces.shape
    return pieces.reshape(*shape[:dim], shape[dim] * shape[dim + 1], *shape[dim + 2 :])


def from_everyone(array, axis):
    size = lax.axis_size(axis)
    return lax.all_to_all(
        jnp.broadcast_to(array[None], (size, *array.shape)), axis, 0, 0, tiled=True
    )


def gathered_copies(array, axis, dim):
    return laid_out(from_everyone(array, axis), dim)


def total_of(array, axes):
    lines = array.reshape(-1, array.shape[-1])
    own = summed_on_arrival(rows_for(lines, lax.axis_size(axes)), axes, 0)
    whole = gathered_copies(own, axes, 0)
    return whole[: len(lines)].reshape(array.shape)


def partner(block, axis, bit):
    count = lax.axis_size(axis)
    route = []
    for low in range(count):
        high = low | 1 << bit
        if high != low and high < count:
            route += [(low, high), (high, low)]
    return lax.ppermute(block, axis, route)


def hdot(left, right):
    return jnp.dot(left, right, precision=lax.Precision.HIGHEST, preferred_element_type=jnp.float32)


def lower_solve(factor, rhs):
    return lax.linalg.triangular_solve(factor, rhs, left_side=True, lower=True)


def rotation(stacked_gram):
    kept = stacked_gram.shape[0] // 2
    subspace = jnp.eye(2 * kept, kept, dtype=jnp.float32)
    product = hdot(stacked_gram, subspace)
    factor = jnp.linalg.cholesky(hdot(product.T, product))
    subspace = lower_solve(factor, product.T).T
    reduced = hdot(subspace.T, hdot(stacked_gram, subspace))
    root_factor = jnp.linalg.cholesky(reduced)
    delta = jnp.trace(reduced) / kept
    damped = jnp.linalg.cholesky(reduced + delta * jnp.eye(kept, dtype=jnp.float32))
    shrunk = lower_solve(damped, reduced)
    whitened = lower_solve(root_factor, subspace.T)
    mixing = hdot(shrunk.T, whitened)
    return (mixing, hdot(shrunk.T, shrunk))


def merge_pair(lower_rows, lower_gram, upper_rows, upper_gram):
    kept = lower_rows.shape[0]
    cross = total_of(hdot(lower_rows, upper_rows.T), "pix")
    stacked_gram = jnp.concatenate(
        [
            jnp.concatenate([lower_gram, cross], axis=1),
            jnp.concatenate([cross.T, upper_gram], axis=1),
        ],
        axis=0,
    )
    mixing, new_gram = rotation(stacked_gram)
    merged = hdot(mixing[:, :kept], lower_rows) + hdot(mixing[:, kept:], upper_rows)
    return (merged, new_gram)


def local(frames):
    kept = frames.shape[0]
    sketch = frames
    sketch_gram = total_of(hdot(frames, frames.T), "pix")
    position = lax.axis_index("frames")
    span = 1 << 0
    other_rows, other_gram = partner((sketch, sketch_gram), "frames", 0)
    is_upper = position // span % 2 == 1
    lower_rows = jnp.where(is_upper, other_rows, sketch)
    upper_rows = jnp.where(is_upper, sketch, other_rows)
    lower_gram = jnp.where(is_upper, other_gram, sketch_gram)
    upper_gram = jnp.where(is_upper, sketch_gram, other_gram)
    sketch, sketch_gram = merge_pair(lower_rows, lower_gram, upper_rows, upper_gram)
    coeffs = total_of(hdot(frames, sketch.T), "pix")
    scaling = 4.0 * kept / (jnp.trace(sketch_gram) + 1e-06)
    projected = hdot(coeffs, sketch) * scaling
    return (sketch, projected)


def solution(mesh):
    return jax.shard_map(
        local,
        mesh=mesh,
        in_specs=(P("frames", "pix"),),
        out_specs=(P(None, "pix"), P("frames", "pix")),
        check_vma=False,
    )
```

profile of v0, /device:TPU:0, one launch (start us, length us, event | category | flops | bytes accessed | tf_op | source)
XLA Modules:
  0.0 173.8 jit_solution(16664541651427764908)
XLA Ops:
  0.6 0.1 collective-permute-start.1
  0.7 1.4 fusion.28
  2.1 21.1 %all_to_all.30 = f32[64,2,128]{2,1,0:T(2,128)S(1)} all-to-all(f32[64,2,128]{2,1,0:T(2,128)S(1)} %bitcast.60), channel_id=1, replica_groups=mesh['frames'=2,'pix'=64] {'pix'}, dimensions={0} | all-to-all | bytes 131072 | tf_op jit(solution)/shard_map/all_to_all | solution.py:14
  23.3 0.1 reduce_sum.43
  23.4 0.7 broadcast_in_dim.12
  24.0 4.9 %all-to-all-start.1 = ((f32[64,2,128]{2,1,0:T(2,128)}), f32[64,2,128]{2,1,0:T(2,128)S(1)}, u32[]{:S(2)}, u32[]{:S(2)}) async-start(f32[64,2,128]{2,1,0:T(2,128)} %broadcast_in_dim.12), calls=%async_computation.1 | async-start | bytes 131072 | tf_op jit(solution)/shard_map/all_to_all | solution.py:33
  29.0 9.6 %all-to-all-done.1 = f32[64,2,128]{2,1,0:T(2,128)S(1)} async-done(((f32[64,2,128]{2,1,0:T(2,128)}), f32[64,2,128]{2,1,0:T(2,128)S(1)}, u32[]{:S(2)}, u32[]{:S(2)}) %all-to-all-start.1) | async-done | bytes 65568 | tf_op jit(solution)/shard_map/all_to_all | solution.py:33
  38.6 0.4 fusion.5
  39.0 14.5 %all_to_all.31 = f32[64,2,128]{2,1,0:T(2,128)S(1)} all-to-all(f32[64,2,128]{2,1,0:T(2,128)S(1)} %bitcast.61), channel_id=1, replica_groups=mesh['frames'=2,'pix'=64] {'pix'}, dimensions={0} | all-to-all | bytes 131072 | tf_op jit(solution)/shard_map/all_to_all | solution.py:14
  53.4 0.1 reduce_sum.44
  53.5 0.7 broadcast_in_dim.13
  54.2 5.1 %all-to-all-start.3 = ((f32[64,2,128]{2,1,0:T(2,128)}), f32[64,2,128]{2,1,0:T(2,128)S(1)}, u32[]{:S(2)}, u32[]{:S(2)}) async-start(f32[64,2,128]{2,1,0:T(2,128)} %broadcast_in_dim.13), calls=%async_computation.3 | async-start | bytes 131072 | tf_op jit(solution)/shard_map/all_to_all | solution.py:33
  59.3 9.4 %all-to-all-done.3 = f32[64,2,128]{2,1,0:T(2,128)S(1)} async-done(((f32[64,2,128]{2,1,0:T(2,128)}), f32[64,2,128]{2,1,0:T(2,128)S(1)}, u32[]{:S(2)}, u32[]{:S(2)}) %all-to-all-start.3) | async-done | bytes 65568 | tf_op jit(solution)/shard_map/all_to_all | solution.py:33
  68.7 0.1 copy.3
  68.8 0.3 fusion.2
  69.1 0.4 fusion.29
  69.5 0.1 copy.4
  69.6 11.7 %cholesky.59 = f32[128,128]{1,0:T(8,128)S(1)} custom-call(f32[128,128]{1,0:T(8,128)S(1)} %fusion.19), custom_call_target="Cholesky" | custom-call | tf_op jit(solution)/shard_map/jit(cholesky)/cholesky | solution.py:71
  81.3 0.6 compare_reduce_fusion.2
  82.0 0.7 fusion.7
  82.6 9.8 %custom-call.10 = f32[1,128,128]{1,2,0:T(8,128)S(1)} custom-call(f32[1,128,128]{2,1,0:T(8,128)S(1)} %fusion.7), custom_call_target="InvertDiagBlocksLowerTriangular" | custom-call | tf_op jit(solution)/shard_map/triangular_solve/custom-call.0 | solution.py:64
  92.4 0.3 fusion.3
  92.8 0.4 fusion.1
  93.1 0.9 fusion.24
  94.0 0.1 copy.7
  94.8 11.7 %cholesky.81 = f32[128,128]{1,0:T(8,128)S(1)} custom-call(f32[128,128]{1,0:T(8,128)S(1)} %get-tuple-element.6), custom_call_target="Cholesky" | custom-call | tf_op jit(solution)/shard_map/jit(cholesky)/cholesky | solution.py:74
  106.5 0.6 compare_reduce_fusion
  107.2 0.7 fusion.9
  107.9 10.0 %custom-call.11 = f32[1,128,128]{1,2,0:T(8,128)S(1)} custom-call(f32[1,128,128]{2,1,0:T(8,128)S(1)} %fusion.9), custom_call_target="InvertDiagBlocksLowerTriangular" | custom-call | tf_op jit(solution)/shard_map/triangular_solve/custom-call.0 | solution.py:64
  117.8 0.3 fusion.12
  118.1 0.1 copy.5
  118.3 0.1 copy.6
  118.4 11.7 %cholesky.70 = f32[128,128]{1,0:T(8,128)S(1)} custom-call(f32[128,128]{1,0:T(8,128)S(1)} %copy.6), custom_call_target="Cholesky" | custom-call | tf_op jit(solution)/shard_map/jit(cholesky)/cholesky | solution.py:76
  130.1 0.6 compare_reduce_fusion.1
  130.8 0.7 fusion.8
  131.4 9.8 %custom-call.8 = f32[1,128,128]{1,2,0:T(8,128)S(1)} custom-call(f32[1,128,128]{2,1,0:T(8,128)S(1)} %fusion.8), custom_call_target="InvertDiagBlocksLowerTriangular" | custom-call | tf_op jit(solution)/shard_map/triangular_solve | solution.py:64
  141.2 0.3 fusion.15
  141.5 0.3 fusion.30
  141.8 0.4 fusion.6
  142.2 0.4 convolution_add_fusion
  142.6 0.4 fusion.31
  143.0 14.5 %all_to_all.32 = f32[64,2,128]{2,1,0:T(2,128)S(1)} all-to-all(f32[64,2,128]{2,1,0:T(2,128)S(1)} %bitcast.62), channel_id=1, replica_groups=mesh['frames'=2,'pix'=64] {'pix'}, dimensions={0} | all-to-all | bytes 131072 | tf_op jit(solution)/shard_map/all_to_all | solution.py:14
  157.5 0.1 reduce_sum.46
  157.6 0.7 broadcast_in_dim.15
  158.2 4.9 %all-to-all-start.5 = ((f32[64,2,128]{2,1,0:T(2,128)}), f32[64,2,128]{2,1,0:T(2,128)S(1)}, u32[]{:S(2)}, u32[]{:S(2)}) async-start(f32[64,2,128]{2,1,0:T(2,128)} %broadcast_in_dim.15), calls=%async_computation.5 | async-start | bytes 131072 | tf_op jit(solution)/shard_map/all_to_all | solution.py:33
  163.2 1.0 fusion
  164.9 7.9 %all-to-all-done.5 = f32[64,2,128]{2,1,0:T(2,128)S(1)} async-done(((f32[64,2,128]{2,1,0:T(2,128)}), f32[64,2,128]{2,1,0:T(2,128)S(1)}, u32[]{:S(2)}, u32[]{:S(2)}) %all-to-all-start.5) | async-done | bytes 65568 | tf_op jit(solution)/shard_map/all_to_all | solution.py:33
  172.8 1.1 convolution_multiply_fusion
  (14 shorter events, 0.2 us)
Async XLA Ops:
  0.6 37.9 %collective-permute-start.1 = (f32[128,512]{1,0:T(8,128)}, f32[128,512]{1,0:T(8,128)S(1)}, u32[]{:S(2)}, u32[]{:S(2)}) collective-permute-start(f32[128,512]{1,0:T(8,128)} %param.4), channel_id=1, source_target_pairs={{0,64},{64,0},{1,65},{65,1},{2,66},{66,2},{3,67},{67,3},{4,68},{68... | collective-permute-start | bytes 786440 | tf_op jit(solution)/shard_map/ppermute | solution.py:56
  2.1 36.4 %copy-start = (f32[128,512]{1,0:T(8,128)S(1)}, f32[128,512]{1,0:T(8,128)}, u32[]{:S(2)}) copy-start(f32[128,512]{1,0:T(8,128)} %param.4) | copy-start | bytes 786436
  24.0 14.5 %all-to-all-start.1 = ((f32[64,2,128]{2,1,0:T(2,128)}), f32[64,2,128]{2,1,0:T(2,128)S(1)}, u32[]{:S(2)}, u32[]{:S(2)}) async-start(f32[64,2,128]{2,1,0:T(2,128)} %broadcast_in_dim.12), calls=%async_computation.1 | async-start | bytes 131072 | tf_op jit(solution)/shard_map/all_to_all | solution.py:33
  38.6 20.7 %collective-permute-start = (f32[128,128]{1,0:T(8,128)S(1)}, f32[128,128]{1,0:T(8,128)S(1)}, u32[]{:S(2)}, u32[]{:S(2)}) collective-permute-start(f32[128,128]{1,0:T(8,128)S(1)} %bitcast.63), channel_id=1, source_target_pairs={{0,64},{64,0},{1,65},{65,1},{2,66},{66,2},{3,67},{67,3},{4,68},{68... | collective-permute-start | bytes 196616 | tf_op jit(solution)/shard_map/ppermute | solution.py:56
  54.2 14.5 %all-to-all-start.3 = ((f32[64,2,128]{2,1,0:T(2,128)}), f32[64,2,128]{2,1,0:T(2,128)S(1)}, u32[]{:S(2)}, u32[]{:S(2)}) async-start(f32[64,2,128]{2,1,0:T(2,128)} %broadcast_in_dim.13), calls=%async_computation.3 | async-start | bytes 131072 | tf_op jit(solution)/shard_map/all_to_all | solution.py:33
  142.6 30.1 %copy-start.1 = (f32[128,512]{1,0:T(8,128)}, f32[128,512]{1,0:T(8,128)S(1)}, u32[]{:S(2)}) copy-start(f32[128,512]{1,0:T(8,128)S(1)} %convolution_add_fusion) | copy-start | bytes 786436
  158.2 14.5 %all-to-all-start.5 = ((f32[64,2,128]{2,1,0:T(2,128)}), f32[64,2,128]{2,1,0:T(2,128)S(1)}, u32[]{:S(2)}, u32[]{:S(2)}) async-start(f32[64,2,128]{2,1,0:T(2,128)} %broadcast_in_dim.15), calls=%async_computation.5 | async-start | bytes 131072 | tf_op jit(solution)/shard_map/all_to_all | solution.py:33
where the time goes:
time: 174 us
  other arithmetic  69 us (40%)
  blocking collectives  50.1 us (29%)
  waiting for transfers between devices  26.8 us (15%)
  starting transfers between devices  15.1 us (9%)
  matrix products  8.08 us (5%)
  local copies, waits for them, and re-layouts  2.4 us (1%)
  between operations  2.31 us (1%)
    all_to_all x3, blocking collectives, summed_on_arrival(): pieces = lax.all_to_all(in_blocks(array, dim, size), axis, 0, 0, tiled=True)  50.1 us
    another operation x6, other arithmetic, lower_solve(): return lax.linalg.triangular_solve(factor, rhs, left_side=True, lower=True)  31.6 us
    all_to_all x3, waiting for transfers between devices, from_everyone(): lax.all_to_all(jnp.broadcast_to(array[None], (size, *array.shape)), axis,...  26.8 us
    all_to_all x3, starting transfers between devices, from_everyone(): lax.all_to_all(jnp.broadcast_to(array[None], (size, *array.shape)), axis,...  15 us
    another operation x3, other arithmetic, rotation(): jnp.linalg.cholesky(reduced + delta * jnp.eye(kept, dtype=jnp.float32))  12.4 us
    another operation x3, other arithmetic, rotation(): factor = jnp.linalg.cholesky(hdot(product.T, product))  12.4 us
    another operation x3, other arithmetic, rotation(): root_factor = jnp.linalg.cholesky(reduced)  12.4 us
    dot_general x12, matrix products, hdot(): jnp.dot(left, right, precision=lax.Precision.HIGHEST, preferred_element_t...  7.17 us
  transfers between devices with their start and end apart: 5, of which 3 were waited for; matrix products, arithmetic and copies ran while one was open for 2% of the time, Pallas kernels for 0%

commit v1 on v0

v1 whole, which is shorter than its diff:
```python
import functools
import jax
import jax.numpy as jnp
from jax import lax
from jax.experimental import pallas as pl
from jax.experimental.pallas import tpu as pltpu
from jax.sharding import PartitionSpec as P

MESH = pl.DeviceIdType.MESH
HI = lax.Precision.HIGHEST
F32 = jnp.float32


def mm(a, b, ca=1, cb=0, prec=HI):
    return lax.dot_general(a, b, (((ca,), (cb,)), ((), ())), precision=prec, preferred_element_type=jnp.float32)

def inverse_factors(mats, PW=32, IB=16):
    n = 128
    lane = lax.broadcasted_iota(jnp.int32, (8, n), 1)
    sub = lax.broadcasted_iota(jnp.int32, (8, n), 0)
    nb = n // 8
    X = [[m[8 * i:8 * i + 8] for i in range(nb)] for m in mats]
    for r0 in range(0, n, PW):
        b0, b1 = r0 // 8, (r0 + PW) // 8
        D = [[None] * nb for _ in mats]
        for i0 in range(r0, r0 + PW, IB):
            ib = i0 // 8
            inner = (lane >= i0) & (lane < i0 + IB)
            CB = [[[None] * nb for _ in range(IB)] for _ in mats]
            for q in range(len(mats)):
                for k in range(IB):
                    for b in range((i0 + k) // 8, b1):
                        CB[q][k][b] = jnp.broadcast_to(X[q][b][:, i0 + k:i0 + k + 1], (8, n))
                for b in range(ib, b1):
                    X[q][b] = jnp.where(inner, jnp.where(lane == sub + 8 * b, 1.0, 0.0), X[q][b])
            for j in range(IB):
                row = i0 + j
                jb, js = row // 8, row % 8
                for q in range(len(mats)):
                    c = CB[q][j]
                    piv = jnp.broadcast_to(c[jb][js:js + 1], (8, n))
                    D[q][jb] = piv if D[q][jb] is None else jnp.where(sub >= js, piv, D[q][jb])
                    r = 1.0 / piv
                    xrow = jnp.broadcast_to(X[q][jb][js:js + 1], (8, n)) * r
                    for k in range(j + 1, IB):
                        kr = i0 + k
                        s = jnp.broadcast_to(c[kr // 8][kr % 8:kr % 8 + 1], (8, n)) * r
                        for b in range(kr // 8, b1):
                            CB[q][k][b] = CB[q][k][b] - c[b] * s
                    for b in range(jb, b1):
                        if b == jb:
                            if js == 7: continue
                            X[q][b] = X[q][b] - jnp.where(sub > js, c[b], 0.0) * xrow
                        else:
                            X[q][b] = X[q][b] - c[b] * xrow
        for q in range(len(mats)):
            for b in range(b0, b1):
                X[q][b] = X[q][b] * lax.rsqrt(D[q][b])
                if IB < PW:
                    X[q][b] = jnp.where((lane > sub + 8 * b) & (lane < r0 + PW), 0.0, X[q][b])
            if b1 < nb:
                U = jnp.concatenate(X[q][b0:b1], axis=0)
                upd = mm(U[:, r0 + PW:], U, 0, 0) if (r0 + PW) % 128 == 0 else mm(U, U, 0, 0)
                off = b1 if upd.shape[0] == n else 0
                panel = (lane >= r0) & (lane < r0 + PW)
                for b in range(b1, nb):
                    X[q][b] = jnp.where(panel, 0.0, X[q][b]) - upd[8 * b:8 * b + 8]
    out = []
    for q in range(len(mats)):
        out.append(jnp.concatenate([jnp.where(lane <= sub + 8 * b, X[q][b], 0.0) for b in range(nb)], axis=0))
    return out

def k2(core_of, opts, gk, gc, stack, sketch_ref, proj_ref):
    core = core_of()
    n = 128
    Ka = gk[0:16].reshape(n, n); Kb = gk[16:32].reshape(n, n); C = gc[...].reshape(n, n)
    N = mm(Ka, Ka) + mm(C, C, 1, 1)
    (Finv,) = inverse_factors([N], **opts)
    Va = mm(Finv, Ka); Vb = mm(Finv, C)
    Ct = C.T
    Ga = mm(Va, Ka) + mm(Vb, Ct)
    Gb = mm(Va, C) + mm(Vb, Kb)
    Hm = mm(Ga, Va, 1, 1) + mm(Gb, Vb, 1, 1)
    ii = lax.broadcasted_iota(jnp.int32, (n, n), 0); jj = lax.broadcasted_iota(jnp.int32, (n, n), 1)
    eye = jnp.where(ii == jj, 1.0, 0.0)
    delta = jnp.sum(Hm * eye, keepdims=True) * (1.0 / n)
    Rinv, Linv = inverse_factors([Hm, Hm + delta * eye], **opts)
    Pm = mm(Linv, Hm)
    Wa = mm(Rinv, Va); Wb = mm(Rinv, Vb)
    Ma = mm(Pm, Wa, 0, 0); Mb = mm(Pm, Wb, 0, 0)
    scale = (4.0 * n) / (jnp.sum(Pm * Pm, keepdims=True) + 1e-06)
    sk = mm(Ma, stack[0]) + mm(Mb, stack[1])
    sketch_ref[...] = sk
    up = core == 1
    L = jnp.where(up, Ct, Ka); R = jnp.where(up, Kb, C)
    co = mm(L, Ma, 1, 1) + mm(R, Mb, 1, 1)
    proj_ref[...] = mm(co * scale, sk)

def call_k2(gk, gc, stack, core_of=lambda: lax.axis_index("frames"), opts=dict(PW=32, IB=16), name="merge_project"):
    V = pl.BlockSpec(memory_space=pltpu.VMEM)
    o = jax.ShapeDtypeStruct((128, 512), jnp.float32)
    return pl.pallas_call(functools.partial(k2, core_of, opts), out_shape=[o, o], in_specs=[V] * 3, out_specs=[V] * 2,
        compiler_params=pltpu.CompilerParams(vmem_limit_bytes=32 << 20), name=name)(gk, gc, stack)


def tree(buf, own, count):
    v = [own] + [buf[d] for d in range(1, count)]
    while len(v) > 1:
        v = [v[i] + v[i + 1] for i in range(0, len(v), 2)]
    return v[0]


def k1(fr, gk, gc, stack, kown, cown, rk, rc, sk, sc, zk, zc, s_ex, r_ex, s_rs, r_rs, s_z, r_z, s_ag, r_ag):
    core = lax.axis_index("frames")
    pix = lax.axis_index("pix")
    z = pix // 16
    p = pix % 16
    bar = pltpu.get_barrier_semaphore()
    greeted = 0
    for d in range(16):
        for e in range(2):
            if d or e:
                pl.semaphore_signal(bar, inc=1, device_id=((core + e) % 2, z * 16 + (p ^ d)), device_id_type=MESH)
                greeted += 1
    for d in range(1, 4):
        pl.semaphore_signal(bar, inc=1, device_id=(core, (z ^ d) * 16 + p), device_id_type=MESH)
        greeted += 1

    def rcopy(src, dst, ss, rs, c, q):
        return pltpu.make_async_remote_copy(src_ref=src, dst_ref=dst, send_sem=ss, recv_sem=rs, device_id=(c, q), device_id_type=MESH)

    mine = fr[...]
    kown[...] = mm(mine, mine, 1, 1).reshape(16, 8, 128)
    stack[core] = mine
    pl.semaphore_wait(bar, greeted)
    ex = rcopy(stack.at[core], stack.at[core], s_ex, r_ex, (core + 1) % 2, pix)
    ex.start()
    for d in range(1, 16):
        rcopy(kown.at[p ^ d], rk.at[d], s_rs.at[0], r_rs.at[0], core, z * 16 + (p ^ d)).start()
    ex.wait()
    half = pl.multiple_of(core * 64, 64)
    cown[...] = mm(stack[0, pl.ds(half, 64), :], stack[1], 1, 1).reshape(16, 4, 128)
    for d in range(1, 16):
        rcopy(cown.at[p ^ d], rc.at[d], s_rs.at[1], r_rs.at[1], core, z * 16 + (p ^ d)).start()

    def wait_for(out, into, ss, rs, count):
        rcopy(out.at[pl.ds(0, count)], into.at[pl.ds(0, count)], ss, rs, (core + 1) % 2, pix).wait()

    wait_for(kown, rk, s_rs.at[0], r_rs.at[0], 15)
    sk[...] = tree(rk, kown[p], 16)
    for d in range(1, 4):
        rcopy(sk, zk.at[d], s_z.at[0], r_z.at[0], core, (z ^ d) * 16 + p).start()
    wait_for(cown, rc, s_rs.at[1], r_rs.at[1], 15)
    sc[...] = tree(rc, cown[p], 16)
    for d in range(1, 4):
        rcopy(sc, zc.at[d], s_z.at[1], r_z.at[1], core, (z ^ d) * 16 + p).start()
    wait_for(kown, zk, s_z.at[0], r_z.at[0], 3)
    gk[core * 16 + p] = tree(zk, sk[...], 4)
    for d in range(16):
        for e in range(2):
            if d or e:
                rcopy(gk.at[core * 16 + p], gk.at[core * 16 + p], s_ag.at[0], r_ag.at[0], (core + e) % 2, z * 16 + (p ^ d)).start()
    wait_for(cown, zc, s_z.at[1], r_z.at[1], 3)
    gc[core * 16 + p] = tree(zc, sc[...], 4)
    for d in range(16):
        for e in range(2):
            if d or e:
                rcopy(gc.at[core * 16 + p], gc.at[core * 16 + p], s_ag.at[1], r_ag.at[1], (core + e) % 2, z * 16 + (p ^ d)).start()
    for i, g in enumerate((gk, gc)):
        wait_for(g, g, s_ag.at[i], r_ag.at[i], 31)


def call_k1(frames):
    vm = pl.BlockSpec(memory_space=pltpu.VMEM)
    dma = pltpu.SemaphoreType.DMA
    return pl.pallas_call(
        k1,
        out_shape=[
            jax.ShapeDtypeStruct((32, 8, 128), F32),
            jax.ShapeDtypeStruct((32, 4, 128), F32),
            jax.ShapeDtypeStruct((2, 128, 512), F32),
        ],
        in_specs=[vm],
        out_specs=[vm] * 3,
        scratch_shapes=[
            pltpu.VMEM((16, 8, 128), F32),
            pltpu.VMEM((16, 4, 128), F32),
            pltpu.VMEM((16, 8, 128), F32),
            pltpu.VMEM((16, 4, 128), F32),
            pltpu.VMEM((8, 128), F32),
            pltpu.VMEM((4, 128), F32),
            pltpu.VMEM((4, 8, 128), F32),
            pltpu.VMEM((4, 4, 128), F32),
            dma(()), dma(()), dma((2,)), dma((2,)), dma((2,)), dma((2,)), dma((2,)), dma((2,)),
        ],
        compiler_params=pltpu.CompilerParams(collective_id=0, has_side_effects=True, vmem_limit_bytes=32 << 20),
        name="gram_exchange",
    )(frames)


def local(frames):
    gk, gc, stack = call_k1(frames)
    return tuple(call_k2(gk, gc, stack))


def solution(mesh):
    return jax.shard_map(
        local,
        mesh=mesh,
        in_specs=(P("frames", "pix"),),
        out_specs=(P(None, "pix"), P("frames", "pix")),
        check_vma=False,
    )
```

time: 174 us -> 37 us (0.21)
  the two profiles are of different devices: /device:TPU:0 before, /device:TPU:1 now
where the time goes in v1:
time: 37 us; the launch traced here: 36.9 us
  Pallas kernels  35.3 us (95%)
  local copies, waits for them, and re-layouts  0.94 us (3%)
  between operations  0.65 us (2%)
    pallas_call x1, Pallas kernels, call_k1(): pl.pallas_call(k1, out_shape=[jax.ShapeDtypeStruct((32, 8, 128), F32), ja...  23.6 us
    pallas_call x1, Pallas kernels, call_k2(): pl.pallas_call(functools.partial(k2, core_of, opts), out_shape=[o, o], in...  11.7 us
    unnamed x2, local copies, waits for them, and re-layouts  0.94 us

profile of v1, /device:TPU:1, one launch (start us, length us, event | category | flops | bytes accessed | tf_op | source)
XLA Modules:
  0.0 36.9 jit_solution(15467134065681359970)
XLA Ops:
  0.6 0.0 copy-start
  0.6 0.9 %copy-done = f32[128,512]{1,0:T(8,128)S(1)} copy-done((f32[128,512]{1,0:T(8,128)S(1)}, f32[128,512]{1,0:T(8,128)}, u32[]{:S(2)}) %copy-start) | copy-done | bytes 262168
  1.6 23.6 %gram_exchange.1 = (f32[32,8,128]{2,1,0:T(8,128)S(1)}, f32[32,4,128]{2,1,0:T(4,128)S(1)}, f32[2,128,512]{2,1,0:T(8,128)S(1)}) custom-call(f32[128,512]{1,0:T(8,128)S(1)} %copy-done), custom_call_target="tpu_custom_call" | custom-call | tf_op jit(solution)/shard_map/gram_exchange/pallas_call | solution.py:176
  25.2 11.7 %merge_project.1 = (f32[128,512]{1,0:T(8,128)}, f32[128,512]{1,0:T(8,128)}) custom-call(f32[32,8,128]{2,1,0:T(8,128)S(1)} %get-tuple-element.5.gk, f32[32,4,128]{2,1,0:T(4,128)S(1)} %get-tuple-element.6.gc, f32[2,128,512]{2,1,0:T(8,128)S(1)} %get-tuple-element.7.stack), custom_call_target="tpu_custom_call" | custom-call | tf_op jit(solution)/shard_map/merge_project/pallas_call | solution.py:102
Async XLA Ops:
  0.6 1.0 %copy-start = (f32[128,512]{1,0:T(8,128)S(1)}, f32[128,512]{1,0:T(8,128)}, u32[]{:S(2)}) copy-start(f32[128,512]{1,0:T(8,128)} %fr.1) | copy-start | bytes 786436

commit v2 on v1

--- a/solution.py
+++ b/solution.py
@@ -73,7 +73,7 @@
 def k2(core_of, opts, gk, gc, stack, sketch_ref, proj_ref):
     core = core_of()
     n = 128
-    Ka = gk[0:16].reshape(n, n); Kb = gk[16:32].reshape(n, n); C = gc[...].reshape(n, n)
+    Ka = gk[0:8].reshape(n, n); Kb = gk[8:16].reshape(n, n); C = gc[...].reshape(n, n)
     N = mm(Ka, Ka) + mm(C, C, 1, 1)
     (Finv,) = inverse_factors([N], **opts)
     Va = mm(Finv, Ka); Vb = mm(Finv, C)
@@ -103,71 +103,79 @@
         compiler_params=pltpu.CompilerParams(vmem_limit_bytes=32 << 20), name=name)(gk, gc, stack)
 
 
-def tree(buf, own, count):
-    v = [own] + [buf[d] for d in range(1, count)]
+def tree(buf, own):
+    v = [own] + [buf[e] for e in range(1, 8)]
     while len(v) > 1:
         v = [v[i] + v[i + 1] for i in range(0, len(v), 2)]
     return v[0]
 
 
-def k1(fr, gk, gc, stack, kown, cown, rk, rc, sk, sc, zk, zc, s_ex, r_ex, s_rs, r_rs, s_z, r_z, s_ag, r_ag):
+NEAR = (7, 6, 5, 3, 4, 2, 1)
+
+
+def step(e, unit):
+    return unit * ((e & 1) + 4 * (e >> 1 & 1) + 16 * (e >> 2))
+
+
+def k1(hbm, gk, gc, stack, kown, cown, rk, rc, sk, sc, zk, zc, s_in, s_ex, r_ex, s_rs, r_rs, s_z, r_z, s_ag, r_ag):
     core = lax.axis_index("frames")
     pix = lax.axis_index("pix")
-    z = pix // 16
-    p = pix % 16
+    partner = (core + 1) % 2
+    load = pltpu.make_async_copy(hbm, stack.at[core], s_in)
+    load.start()
+    bit = lambda t: (t % 4 + 1) // 2 % 2
+    own = bit(pix) + 2 * bit(pix // 4) + 4 * bit(pix // 16)
+    mates = [((core + f) % 2, pix ^ step(e, 1)) for e in NEAR + (0,) for f in (0, 1) if e or f]
+    others = [(core, pix ^ step(e, 3)) for e in NEAR]
     bar = pltpu.get_barrier_semaphore()
-    greeted = 0
-    for d in range(16):
-        for e in range(2):
-            if d or e:
-                pl.semaphore_signal(bar, inc=1, device_id=((core + e) % 2, z * 16 + (p ^ d)), device_id_type=MESH)
-                greeted += 1
-    for d in range(1, 4):
-        pl.semaphore_signal(bar, inc=1, device_id=(core, (z ^ d) * 16 + p), device_id_type=MESH)
-        greeted += 1
-
-    def rcopy(src, dst, ss, rs, c, q):
-        return pltpu.make_async_remote_copy(src_ref=src, dst_ref=dst, send_sem=ss, recv_sem=rs, device_id=(c, q), device_id_type=MESH)
-
-    mine = fr[...]
-    kown[...] = mm(mine, mine, 1, 1).reshape(16, 8, 128)
-    stack[core] = mine
-    pl.semaphore_wait(bar, greeted)
-    ex = rcopy(stack.at[core], stack.at[core], s_ex, r_ex, (core + 1) % 2, pix)
+    for device in others + mates:
+        pl.semaphore_signal(bar, inc=1, device_id=device, device_id_type=MESH)
+
+    def rcopy(src, dst, ss, rs, device):
+        return pltpu.make_async_remote_copy(src_ref=src, dst_ref=dst, send_sem=ss, recv_sem=rs, device_id=device, device_id_type=MESH)
+
+    load.wait()
+    mine = stack[core]
+    kown[...] = mm(mine, mine, 1, 1).reshape(8, 16, 128)
+    pl.semaphore_wait(bar, len(others + mates))
+    ex = rcopy(stack.at[core], stack.at[core], s_ex, r_ex, (partner, pix))
     ex.start()
-    for d in range(1, 16):
-        rcopy(kown.at[p ^ d], rk.at[d], s_rs.at[0], r_rs.at[0], core, z * 16 + (p ^ d)).start()
+
+    def scatter(block, into, i):
+        for e in NEAR:
+            rcopy(block.at[own ^ e], into.at[e], s_rs.at[i], r_rs.at[i], (core, pix ^ step(e, 1))).start()
+
+    def across(block, into, i):
+        for e in NEAR:
+            rcopy(block, into.at[e], s_z.at[i], r_z.at[i], (core, pix ^ step(e, 3))).start()
+
+    def gather(g, i):
+        for device in mates:
+            rcopy(g.at[core * 8 + own], g.at[core * 8 + own], s_ag.at[i], r_ag.at[i], device).start()
+
+    def wait_for(buf, ss, rs, count):
+        some = buf.at[pl.ds(0, count)]
+        rcopy(some, some, ss, rs, (partner, pix)).wait()
+
+    scatter(kown, rk, 0)
     ex.wait()
     half = pl.multiple_of(core * 64, 64)
-    cown[...] = mm(stack[0, pl.ds(half, 64), :], stack[1], 1, 1).reshape(16, 4, 128)
-    for d in range(1, 16):
-        rcopy(cown.at[p ^ d], rc.at[d], s_rs.at[1], r_rs.at[1], core, z * 16 + (p ^ d)).start()
-
-    def wait_for(out, into, ss, rs, count):
-        rcopy(out.at[pl.ds(0, count)], into.at[pl.ds(0, count)], ss, rs, (core + 1) % 2, pix).wait()
-
-    wait_for(kown, rk, s_rs.at[0], r_rs.at[0], 15)
-    sk[...] = tree(rk, kown[p], 16)
-    for d in range(1, 4):
-        rcopy(sk, zk.at[d], s_z.at[0], r_z.at[0], core, (z ^ d) * 16 + p).start()
-    wait_for(cown, rc, s_rs.at[1], r_rs.at[1], 15)
-    sc[...] = tree(rc, cown[p], 16)
-    for d in range(1, 4):
-        rcopy(sc, zc.at[d], s_z.at[1], r_z.at[1], core, (z ^ d) * 16 + p).start()
-    wait_for(kown, zk, s_z.at[0], r_z.at[0], 3)
-    gk[core * 16 + p] = tree(zk, sk[...], 4)
-    for d in range(16):
-        for e in range(2):
-            if d or e:
-                rcopy(gk.at[core * 16 + p], gk.at[core * 16 + p], s_ag.at[0], r_ag.at[0], (core + e) % 2, z * 16 + (p ^ d)).start()
-    wait_for(cown, zc, s_z.at[1], r_z.at[1], 3)
-    gc[core * 16 + p] = tree(zc, sc[...], 4)
-    for d in range(16):
-        for e in range(2):
-            if d or e:
-                rcopy(gc.at[core * 16 + p], gc.at[core * 16 + p], s_ag.at[1], r_ag.at[1], (core + e) % 2, z * 16 + (p ^ d)).start()
-    for i, g in enumerate((gk, gc)):
-        wait_for(g, g, s_ag.at[i], r_ag.at[i], 31)
+    cown[...] = mm(stack[0, pl.ds(half, 64), :], stack[1], 1, 1).reshape(8, 8, 128)
+    scatter(cown, rc, 1)
+    wait_for(rk, s_rs.at[0], r_rs.at[0], 7)
+    sk[...] = tree(rk, kown[own])
+    across(sk, zk, 0)
+    wait_for(rc, s_rs.at[1], r_rs.at[1], 7)
+    sc[...] = tree(rc, cown[own])
+    across(sc, zc, 1)
+    wait_for(zk, s_z.at[0], r_z.at[0], 7)
+    gk[core * 8 + own] = tree(zk, sk[...])
+    gather(gk, 0)
+    wait_for(zc, s_z.at[1], r_z.at[1], 7)
+    gc[core * 8 + own] = tree(zc, sc[...])
+    gather(gc, 1)
+    wait_for(gk, s_ag.at[0], r_ag.at[0], 15)
+    wait_for(gc, s_ag.at[1], r_ag.at[1], 15)
 
 
 def call_k1(frames):
@@ -176,22 +184,22 @@
     return pl.pallas_call(
         k1,
         out_shape=[
-            jax.ShapeDtypeStruct((32, 8, 128), F32),
-            jax.ShapeDtypeStruct((32, 4, 128), F32),
+            jax.ShapeDtypeStruct((16, 16, 128), F32),
+            jax.ShapeDtypeStruct((16, 8, 128), F32),
             jax.ShapeDtypeStruct((2, 128, 512), F32),
         ],
-        in_specs=[vm],
+        in_specs=[pl.BlockSpec(memory_space=pltpu.HBM)],
         out_specs=[vm] * 3,
         scratch_shapes=[
-            pltpu.VMEM((16, 8, 128), F32),
-            pltpu.VMEM((16, 4, 128), F32),
-            pltpu.VMEM((16, 8, 128), F32),
-            pltpu.VMEM((16, 4, 128), F32),
+            pltpu.VMEM((8, 16, 128), F32),
+            pltpu.VMEM((8, 8, 128), F32),
+            pltpu.VMEM((8, 16, 128), F32),
+            pltpu.VMEM((8, 8, 128), F32),
+            pltpu.VMEM((16, 128), F32),
             pltpu.VMEM((8, 128), F32),
-            pltpu.VMEM((4, 128), F32),
-            pltpu.VMEM((4, 8, 128), F32),
-            pltpu.VMEM((4, 4, 128), F32),
-            dma(()), dma(()), dma((2,)), dma((2,)), dma((2,)), dma((2,)), dma((2,)), dma((2,)),
+            pltpu.VMEM((8, 16, 128), F32),
+            pltpu.VMEM((8, 8, 128), F32),
+            dma(()), dma(()), dma(()), dma((2,)), dma((2,)), dma((2,)), dma((2,)), dma((2,)), dma((2,)),
         ],
         compiler_params=pltpu.CompilerParams(collective_id=0, has_side_effects=True, vmem_limit_bytes=32 << 20),
         name="gram_exchange",
@@ -199,7 +207,7 @@
 
 
 def local(frames):
-    gk, gc, stack = call_k1(frames)
+    gk, gc, stack = call_k1(pltpu.with_memory_space_constraint(frames, pltpu.HBM))
     return tuple(call_k2(gk, gc, stack))
 
 

time: 37 us -> 33.3 us (0.90)
  Pallas kernels: 35.3 us -> 32.5 us
  local copies, waits for them, and re-layouts: 0.94 us -> 0 us
    pallas_call x1, Pallas kernels: 23.6 us -> 20.9 us  [call_k1(): pl.pallas_call(k1, out_shape=[jax.ShapeDtypeStruct((16, 16, 128), F32), j...]
    unnamed x2 -> x0, local copies, waits for them, and re-layouts: 0.94 us -> none
where the time goes in v2:
time: 33.3 us; the launch traced here: 33.2 us
  Pallas kernels  32.5 us (98%)
  between operations  0.64 us (2%)
    pallas_call x1, Pallas kernels, call_k1(): pl.pallas_call(k1, out_shape=[jax.ShapeDtypeStruct((16, 16, 128), F32), j...  20.9 us
    pallas_call x1, Pallas kernels, call_k2(): pl.pallas_call(functools.partial(k2, core_of, opts), out_shape=[o, o], in...  11.7 us

profile of v2, /device:TPU:1, one launch (start us, length us, event | category | flops | bytes accessed | tf_op | source)
XLA Modules:
  0.0 33.2 jit_solution(7206564439847666993)
XLA Ops:
  0.6 20.9 %gram_exchange.1 = (f32[16,16,128]{2,1,0:T(8,128)S(1)}, f32[16,8,128]{2,1,0:T(8,128)S(1)}, f32[2,128,512]{2,1,0:T(8,128)S(1)}) custom-call(f32[128,512]{1,0:T(8,128)} %hbm.1), custom_call_target="tpu_custom_call" | custom-call | tf_op jit(solution)/shard_map/gram_exchange/pallas_call | solution.py:184
  21.5 11.7 %merge_project.1 = (f32[128,512]{1,0:T(8,128)}, f32[128,512]{1,0:T(8,128)}) custom-call(f32[16,16,128]{2,1,0:T(8,128)S(1)} %get-tuple-element.5.gk, f32[16,8,128]{2,1,0:T(8,128)S(1)} %get-tuple-element.6.gc, f32[2,128,512]{2,1,0:T(8,128)S(1)} %get-tuple-element.7.stack), custom_call_target="tpu_custom_call" | custom-call | tf_op jit(solution)/shard_map/merge_project/pallas_call | solution.py:102

commit v3 on v2

--- a/solution.py
+++ b/solution.py
@@ -70,36 +70,47 @@
         out.append(jnp.concatenate([jnp.where(lane <= sub + 8 * b, X[q][b], 0.0) for b in range(nb)], axis=0))
     return out
 
-def k2(core_of, opts, gk, gc, stack, sketch_ref, proj_ref):
+def k2(core_of, opts, gk, gc, stack, sketch_hbm, proj_hbm, sketch, proj, sem):
     core = core_of()
     n = 128
-    Ka = gk[0:8].reshape(n, n); Kb = gk[8:16].reshape(n, n); C = gc[...].reshape(n, n)
-    N = mm(Ka, Ka) + mm(C, C, 1, 1)
+    Ka = gk[0:8].reshape(n, n)
+    Kb = gk[8:16].reshape(n, n)
+    C = gc[...].reshape(n, n)
+    WT = jnp.concatenate([Ka, C], axis=1)
+    N = mm(WT, WT, 1, 1)
+    Z = mm(WT, jnp.concatenate([WT, jnp.concatenate([C.T, Kb], axis=1)], axis=0))
     (Finv,) = inverse_factors([N], **opts)
-    Va = mm(Finv, Ka); Vb = mm(Finv, C)
-    Ct = C.T
-    Ga = mm(Va, Ka) + mm(Vb, Ct)
-    Gb = mm(Va, C) + mm(Vb, Kb)
-    Hm = mm(Ga, Va, 1, 1) + mm(Gb, Vb, 1, 1)
-    ii = lax.broadcasted_iota(jnp.int32, (n, n), 0); jj = lax.broadcasted_iota(jnp.int32, (n, n), 1)
-    eye = jnp.where(ii == jj, 1.0, 0.0)
-    delta = jnp.sum(Hm * eye, keepdims=True) * (1.0 / n)
-    Rinv, Linv = inverse_factors([Hm, Hm + delta * eye], **opts)
-    Pm = mm(Linv, Hm)
-    Wa = mm(Rinv, Va); Wb = mm(Rinv, Vb)
-    Ma = mm(Pm, Wa, 0, 0); Mb = mm(Pm, Wb, 0, 0)
-    scale = (4.0 * n) / (jnp.sum(Pm * Pm, keepdims=True) + 1e-06)
-    sk = mm(Ma, stack[0]) + mm(Mb, stack[1])
-    sketch_ref[...] = sk
-    up = core == 1
-    L = jnp.where(up, Ct, Ka); R = jnp.where(up, Kb, C)
-    co = mm(L, Ma, 1, 1) + mm(R, Mb, 1, 1)
-    proj_ref[...] = mm(co * scale, sk)
+    VT = mm(Finv, WT)
+    VG = mm(Finv, Z)
+    H = mm(VG, VT, 1, 1)
+    delta = jnp.sum(jnp.sum(VG * VT, axis=0, keepdims=True), axis=1, keepdims=True) * (1.0 / n)
+    ii = lax.broadcasted_iota(jnp.int32, (n, n), 0)
+    jj = lax.broadcasted_iota(jnp.int32, (n, n), 1)
+    VF = mm(VT, stack[...].reshape(2 * n, stack.shape[2]))
+    GV = jnp.where(core == 1, VG[:, n:], VG[:, :n]).T
+    Rinv, Linv = inverse_factors([H, H + jnp.where(ii == jj, delta, 0.0)], **opts)
+    WF = mm(Rinv, VF)
+    PT = mm(H, Linv, 1, 1)
+    Pm = mm(Linv, H)
+    YT = mm(GV, Rinv, 1, 1)
+    sk = mm(PT, WF)
+    sketch[...] = sk
+    out = pltpu.make_async_copy(sketch, sketch_hbm, sem.at[0])
+    out.start()
+    co = mm(YT, Pm)
+    gram_trace = jnp.sum(jnp.sum(Pm * Pm, axis=0, keepdims=True), axis=1, keepdims=True)
+    proj[...] = mm(co * ((4.0 * n) / (gram_trace + 1e-06)), sk)
+    last = pltpu.make_async_copy(proj, proj_hbm, sem.at[1])
+    last.start()
+    out.wait()
+    last.wait()
+
 
 def call_k2(gk, gc, stack, core_of=lambda: lax.axis_index("frames"), opts=dict(PW=32, IB=16), name="merge_project"):
     V = pl.BlockSpec(memory_space=pltpu.VMEM)
     o = jax.ShapeDtypeStruct((128, 512), jnp.float32)
-    return pl.pallas_call(functools.partial(k2, core_of, opts), out_shape=[o, o], in_specs=[V] * 3, out_specs=[V] * 2,
+    return pl.pallas_call(functools.partial(k2, core_of, opts), out_shape=[o, o], in_specs=[V] * 3, out_specs=[pl.BlockSpec(memory_space=pltpu.HBM)] * 2,
+        scratch_shapes=[pltpu.VMEM((128, 512), jnp.float32)] * 2 + [pltpu.SemaphoreType.DMA((2,))],
         compiler_params=pltpu.CompilerParams(vmem_limit_bytes=32 << 20), name=name)(gk, gc, stack)
 
 

time: 33.3 us -> 31.9 us (0.958)
  Pallas kernels: 32.5 us -> 31.1 us
    pallas_call x1, Pallas kernels: 11.7 us -> 10.3 us  [call_k2(): pl.pallas_call(functools.partial(k2, core_of, opts), out_shape=[o, o], in...]
where the time goes in v3:
time: 31.9 us; the launch traced here: 31.8 us
  Pallas kernels  31.1 us (97%)
  between operations  0.64 us (2%)
    pallas_call x1, Pallas kernels, call_k1(): pl.pallas_call(k1, out_shape=[jax.ShapeDtypeStruct((16, 16, 128), F32), j...  20.9 us
    pallas_call x1, Pallas kernels, call_k2(): pl.pallas_call(functools.partial(k2, core_of, opts), out_shape=[o, o], in...  10.3 us

profile of v3, /device:TPU:1, one launch (start us, length us, event | category | flops | bytes accessed | tf_op | source)
XLA Modules:
  0.0 31.8 jit_solution(5693561084721031362)
XLA Ops:
  0.6 20.9 %gram_exchange.1 = (f32[16,16,128]{2,1,0:T(8,128)S(1)}, f32[16,8,128]{2,1,0:T(8,128)S(1)}, f32[2,128,512]{2,1,0:T(8,128)S(1)}) custom-call(f32[128,512]{1,0:T(8,128)} %hbm.1), custom_call_target="tpu_custom_call" | custom-call | tf_op jit(solution)/shard_map/gram_exchange/pallas_call | solution.py:195
  21.5 10.3 %merge_project.1 = (f32[128,512]{1,0:T(8,128)}, f32[128,512]{1,0:T(8,128)}) custom-call(f32[16,16,128]{2,1,0:T(8,128)S(1)} %get-tuple-element.5.gk, f32[16,8,128]{2,1,0:T(8,128)S(1)} %get-tuple-element.6.gc, f32[2,128,512]{2,1,0:T(8,128)S(1)} %get-tuple-element.7.stack), custom_call_target="tpu_custom_call" | custom-call | tf_op jit(solution)/shard_map/merge_project/pallas_call | solution.py:112

commit v4 on v3

--- a/solution.py
+++ b/solution.py
@@ -10,11 +10,12 @@
 HI = lax.Precision.HIGHEST
 F32 = jnp.float32
 
+MID = lax.Precision.HIGH
 
 def mm(a, b, ca=1, cb=0, prec=HI):
     return lax.dot_general(a, b, (((ca,), (cb,)), ((), ())), precision=prec, preferred_element_type=jnp.float32)
 
-def inverse_factors(mats, PW=32, IB=16):
+def inverse_factors(mats, PW=64, IB=16):
     n = 128
     lane = lax.broadcasted_iota(jnp.int32, (8, n), 1)
     sub = lax.broadcasted_iota(jnp.int32, (8, n), 0)
@@ -41,18 +42,19 @@
                     piv = jnp.broadcast_to(c[jb][js:js + 1], (8, n))
                     D[q][jb] = piv if D[q][jb] is None else jnp.where(sub >= js, piv, D[q][jb])
                     r = 1.0 / piv
-                    xrow = jnp.broadcast_to(X[q][jb][js:js + 1], (8, n)) * r
+                    xrow = jnp.broadcast_to(X[q][jb][js:js + 1], (8, n))
+                    m = [None if b < jb or b >= b1 else c[b] * r for b in range(nb)]
                     for k in range(j + 1, IB):
                         kr = i0 + k
-                        s = jnp.broadcast_to(c[kr // 8][kr % 8:kr % 8 + 1], (8, n)) * r
+                        s = jnp.broadcast_to(c[kr // 8][kr % 8:kr % 8 + 1], (8, n))
                         for b in range(kr // 8, b1):
-                            CB[q][k][b] = CB[q][k][b] - c[b] * s
+                            CB[q][k][b] = CB[q][k][b] - m[b] * s
                     for b in range(jb, b1):
                         if b == jb:
                             if js == 7: continue
-                            X[q][b] = X[q][b] - jnp.where(sub > js, c[b], 0.0) * xrow
+                            X[q][b] = X[q][b] - jnp.where(sub > js, m[b], 0.0) * xrow
                         else:
-                            X[q][b] = X[q][b] - c[b] * xrow
+                            X[q][b] = X[q][b] - m[b] * xrow
         for q in range(len(mats)):
             for b in range(b0, b1):
                 X[q][b] = X[q][b] * lax.rsqrt(D[q][b])
@@ -70,6 +72,80 @@
         out.append(jnp.concatenate([jnp.where(lane <= sub + 8 * b, X[q][b], 0.0) for b in range(nb)], axis=0))
     return out
 
+def inverse_pair(Y, PW=64, IB=16):
+    n = 128
+    lane = lax.broadcasted_iota(jnp.int32, (8, n), 1)
+    sub = lax.broadcasted_iota(jnp.int32, (8, n), 0)
+    first = lane < 64
+    col = jnp.where(first, lane, lane - 64)
+    nb = n // 8
+    X = [[Y[8 * b:8 * b + 8, n * t:n * t + n] for b in range(nb)] for t in range(2)]
+    for r0 in range(0, n, PW):
+        b0, b1 = r0 // 8, (r0 + PW) // 8
+        D = [None] * nb
+        for i0 in range(r0, r0 + PW, IB):
+            ib = i0 // 8
+            CB = [[None] * nb for _ in range(IB)]
+            for k in range(IB):
+                t, w = (i0 + k) // 64, (i0 + k) % 64
+                for b in range((i0 + k) // 8, b1):
+                    CB[k][b] = jnp.where(first, jnp.broadcast_to(X[t][b][:, w:w + 1], (8, n)), jnp.broadcast_to(X[t][b][:, 64 + w:65 + w], (8, n)))
+            t, w = i0 // 64, i0 % 64
+            inner = (col >= w) & (col < w + IB)
+            for b in range(ib, b1):
+                X[t][b] = jnp.where(inner, jnp.where(col + 64 * t == sub + 8 * b, 1.0, 0.0), X[t][b])
+            for j in range(IB):
+                row = i0 + j
+                jb, js = row // 8, row % 8
+                c = CB[j]
+                piv = jnp.broadcast_to(c[jb][js:js + 1], (8, n))
+                D[jb] = piv if D[jb] is None else jnp.where(sub >= js, piv, D[jb])
+                r = 1.0 / piv
+                xrow = [jnp.broadcast_to(X[t][jb][js:js + 1], (8, n)) for t in range(2)]
+                m = [None if b < jb or b >= b1 else c[b] * r for b in range(nb)]
+                for k in range(j + 1, IB):
+                    kr = i0 + k
+                    s = jnp.broadcast_to(c[kr // 8][kr % 8:kr % 8 + 1], (8, n))
+                    for b in range(kr // 8, b1):
+                        CB[k][b] = CB[k][b] - m[b] * s
+                for b in range(jb, b1):
+                    if b == jb and js == 7: continue
+                    f = jnp.where(sub > js, m[b], 0.0) if b == jb else m[b]
+                    for t in range(2):
+                        X[t][b] = X[t][b] - f * xrow[t]
+        tp, wp = r0 // 64, r0 % 64
+        for b in range(b0, b1):
+            sc = lax.rsqrt(D[b])
+            for t in range(2):
+                X[t][b] = X[t][b] * sc
+            X[tp][b] = jnp.where((col + 64 * tp > sub + 8 * b) & (col < wp + PW), 0.0, X[tp][b])
+        if b1 < nb:
+            U = [jnp.concatenate(X[t][b0:b1], axis=0) for t in range(2)]
+            both = jnp.concatenate(U, axis=1)
+            upd = [mm(U[t], both, 0, 0) if r0 + PW < 64 * t + 64 else None for t in range(2)]
+            panel = (col >= wp) & (col < wp + PW)
+            for b in range(b1, nb):
+                u, g = upd[b // 8], 8 * (b % 8)
+                for t in range(2):
+                    old = jnp.where(panel, 0.0, X[t][b]) if t == tp else X[t][b]
+                    X[t][b] = old - jnp.where(first, u[g:g + 8, n * t:n * t + n], u[64 + g:72 + g, n * t:n * t + n])
+    for b in range(nb):
+        X[b // 8][b] = jnp.where(col + 64 * (b // 8) <= sub + 8 * b, X[b // 8][b], 0.0)
+        if b < 8:
+            X[1][b] = jnp.zeros((8, n), jnp.float32)
+    return jnp.concatenate([jnp.concatenate(X[t], axis=0) for t in range(2)], axis=1)
+
+
+def doubled(rows):
+    return jnp.concatenate([rows[:64], rows[:64], rows[64:], rows[64:]], axis=0)
+
+
+def interleaved(rows, second):
+    z = jnp.zeros((64, rows.shape[1]), jnp.float32)
+    parts = [z, rows[:64], z, rows[64:]] if second else [rows[:64], z, rows[64:], z]
+    return jnp.concatenate(parts, axis=0)
+
+
 def k2(core_of, opts, gk, gc, stack, sketch_hbm, proj_hbm, sketch, proj, sem):
     core = core_of()
     n = 128
@@ -82,31 +158,35 @@
     (Finv,) = inverse_factors([N], **opts)
     VT = mm(Finv, WT)
     VG = mm(Finv, Z)
+    V2 = doubled(VT)
     H = mm(VG, VT, 1, 1)
+    H2 = mm(VG, V2, 1, 1)
     delta = jnp.sum(jnp.sum(VG * VT, axis=0, keepdims=True), axis=1, keepdims=True) * (1.0 / n)
-    ii = lax.broadcasted_iota(jnp.int32, (n, n), 0)
-    jj = lax.broadcasted_iota(jnp.int32, (n, n), 1)
-    VF = mm(VT, stack[...].reshape(2 * n, stack.shape[2]))
-    GV = jnp.where(core == 1, VG[:, n:], VG[:, :n]).T
-    Rinv, Linv = inverse_factors([H, H + jnp.where(ii == jj, delta, 0.0)], **opts)
-    WF = mm(Rinv, VF)
-    PT = mm(H, Linv, 1, 1)
-    Pm = mm(Linv, H)
-    YT = mm(GV, Rinv, 1, 1)
-    sk = mm(PT, WF)
+    ii = lax.broadcasted_iota(jnp.int32, (n, 2 * n), 0)
+    jj = lax.broadcasted_iota(jnp.int32, (n, 2 * n), 1)
+    second = jj % n >= 64
+    VF = interleaved(mm(VT, stack[...].reshape(2 * n, stack.shape[2])), False)
+    own = jnp.where(core == 1, jnp.concatenate([C.T, Kb], axis=1), WT)
+    GV = jnp.where(second, 0.0, mm(own, V2, 1, 1))
+    both = inverse_pair(H2 + jnp.where(second & (ii == jj % 64 + 64 * (jj // n)), delta, 0.0), **opts)
+    WF = mm(both, VF)
+    PT = mm(jnp.where(second, H2, 0.0), both, 1, 1, MID)
+    Pm = mm(both, interleaved(H, True), prec=MID)
+    YT = mm(GV, both, 1, 1)
+    sk = mm(PT, WF, prec=MID)
     sketch[...] = sk
     out = pltpu.make_async_copy(sketch, sketch_hbm, sem.at[0])
     out.start()
-    co = mm(YT, Pm)
+    co = mm(YT, Pm, prec=MID)
     gram_trace = jnp.sum(jnp.sum(Pm * Pm, axis=0, keepdims=True), axis=1, keepdims=True)
-    proj[...] = mm(co * ((4.0 * n) / (gram_trace + 1e-06)), sk)
+    proj[...] = mm(co * ((4.0 * n) / (gram_trace + 1e-06)), sk, prec=MID)
     last = pltpu.make_async_copy(proj, proj_hbm, sem.at[1])
     last.start()
     out.wait()
     last.wait()
 
 
-def call_k2(gk, gc, stack, core_of=lambda: lax.axis_index("frames"), opts=dict(PW=32, IB=16), name="merge_project"):
+def call_k2(gk, gc, stack, core_of=lambda: lax.axis_index("frames"), opts=dict(PW=64, IB=16), name="merge_project"):
     V = pl.BlockSpec(memory_space=pltpu.VMEM)
     o = jax.ShapeDtypeStruct((128, 512), jnp.float32)
     return pl.pallas_call(functools.partial(k2, core_of, opts), out_shape=[o, o], in_specs=[V] * 3, out_specs=[pl.BlockSpec(memory_space=pltpu.HBM)] * 2,

time: 31.9 us -> 30.6 us (0.959)
  Pallas kernels: 31.1 us -> 29.9 us
    pallas_call x1, Pallas kernels: 10.3 us -> 8.97 us  [call_k2(): pl.pallas_call(functools.partial(k2, core_of, opts), out_shape=[o, o], in...]
where the time goes in v4:
time: 30.6 us; the launch traced here: 30.5 us
  Pallas kernels  29.9 us (98%)
  between operations  0.64 us (2%)
    pallas_call x1, Pallas kernels, call_k1(): pl.pallas_call(k1, out_shape=[jax.ShapeDtypeStruct((16, 16, 128), F32), j...  20.9 us
    pallas_call x1, Pallas kernels, call_k2(): pl.pallas_call(functools.partial(k2, core_of, opts), out_shape=[o, o], in...  8.97 us

profile of v4, /device:TPU:1, one launch (start us, length us, event | category | flops | bytes accessed | tf_op | source)
XLA Modules:
  0.0 30.5 jit_solution(5995048622968940604)
XLA Ops:
  0.6 20.9 %gram_exchange.1 = (f32[16,16,128]{2,1,0:T(8,128)S(1)}, f32[16,8,128]{2,1,0:T(8,128)S(1)}, f32[2,128,512]{2,1,0:T(8,128)S(1)}) custom-call(f32[128,512]{1,0:T(8,128)} %hbm.1), custom_call_target="tpu_custom_call" | custom-call | tf_op jit(solution)/shard_map/gram_exchange/pallas_call | solution.py:275
  21.5 9.0 %merge_project.1 = (f32[128,512]{1,0:T(8,128)}, f32[128,512]{1,0:T(8,128)}) custom-call(f32[16,16,128]{2,1,0:T(8,128)S(1)} %get-tuple-element.5.gk, f32[16,8,128]{2,1,0:T(8,128)S(1)} %get-tuple-element.6.gc, f32[2,128,512]{2,1,0:T(8,128)S(1)} %get-tuple-element.7.stack), custom_call_target="tpu_custom_call" | custom-call | tf_op jit(solution)/shard_map/merge_project/pallas_call | solution.py:192

commit v5 on v4

--- a/solution.py
+++ b/solution.py
@@ -29,9 +29,11 @@
             inner = (lane >= i0) & (lane < i0 + IB)
             CB = [[[None] * nb for _ in range(IB)] for _ in mats]
             for q in range(len(mats)):
-                for k in range(IB):
-                    for b in range((i0 + k) // 8, b1):
-                        CB[q][k][b] = jnp.broadcast_to(X[q][b][:, i0 + k:i0 + k + 1], (8, n))
+                for near in (True, False):
+                    for k in range(IB):
+                        for b in range((i0 + k) // 8, b1):
+                            if (b < ib + IB // 8) == near:
+                                CB[q][k][b] = jnp.broadcast_to(X[q][b][:, i0 + k:i0 + k + 1], (8, n))
                 for b in range(ib, b1):
                     X[q][b] = jnp.where(inner, jnp.where(lane == sub + 8 * b, 1.0, 0.0), X[q][b])
             for j in range(IB):
@@ -86,10 +88,12 @@
         for i0 in range(r0, r0 + PW, IB):
             ib = i0 // 8
             CB = [[None] * nb for _ in range(IB)]
-            for k in range(IB):
-                t, w = (i0 + k) // 64, (i0 + k) % 64
-                for b in range((i0 + k) // 8, b1):
-                    CB[k][b] = jnp.where(first, jnp.broadcast_to(X[t][b][:, w:w + 1], (8, n)), jnp.broadcast_to(X[t][b][:, 64 + w:65 + w], (8, n)))
+            for near in (True, False):
+                for k in range(IB):
+                    t, w = (i0 + k) // 64, (i0 + k) % 64
+                    for b in range((i0 + k) // 8, b1):
+                        if (b < ib + IB // 8) == near:
+                            CB[k][b] = jnp.where(first, jnp.broadcast_to(X[t][b][:, w:w + 1], (8, n)), jnp.broadcast_to(X[t][b][:, 64 + w:65 + w], (8, n)))
             t, w = i0 // 64, i0 % 64
             inner = (col >= w) & (col < w + IB)
             for b in range(ib, b1):
@@ -179,18 +183,24 @@
     out.start()
     co = mm(YT, Pm, prec=MID)
     gram_trace = jnp.sum(jnp.sum(Pm * Pm, axis=0, keepdims=True), axis=1, keepdims=True)
-    proj[...] = mm(co * ((4.0 * n) / (gram_trace + 1e-06)), sk, prec=MID)
-    last = pltpu.make_async_copy(proj, proj_hbm, sem.at[1])
-    last.start()
+    scaled = co * ((4.0 * n) / (gram_trace + 1e-06))
+    parts = []
+    for i in range(2):
+        cols = pl.ds(256 * i, 256)
+        proj[:, cols] = mm(scaled, sk[:, 256 * i:256 * i + 256], prec=MID)
+        part = pltpu.make_async_copy(proj.at[:, cols], proj_hbm.at[:, cols], sem.at[1 + i])
+        part.start()
+        parts.append(part)
     out.wait()
-    last.wait()
+    for part in parts:
+        part.wait()
 
 
 def call_k2(gk, gc, stack, core_of=lambda: lax.axis_index("frames"), opts=dict(PW=64, IB=16), name="merge_project"):
     V = pl.BlockSpec(memory_space=pltpu.VMEM)
     o = jax.ShapeDtypeStruct((128, 512), jnp.float32)
     return pl.pallas_call(functools.partial(k2, core_of, opts), out_shape=[o, o], in_specs=[V] * 3, out_specs=[pl.BlockSpec(memory_space=pltpu.HBM)] * 2,
-        scratch_shapes=[pltpu.VMEM((128, 512), jnp.float32)] * 2 + [pltpu.SemaphoreType.DMA((2,))],
+        scratch_shapes=[pltpu.VMEM((128, 512), jnp.float32)] * 2 + [pltpu.SemaphoreType.DMA((3,))],
         compiler_params=pltpu.CompilerParams(vmem_limit_bytes=32 << 20), name=name)(gk, gc, stack)
 
 
@@ -208,7 +218,7 @@
     return unit * ((e & 1) + 4 * (e >> 1 & 1) + 16 * (e >> 2))
 
 
-def k1(hbm, gk, gc, stack, kown, cown, rk, rc, sk, sc, zk, zc, s_in, s_ex, r_ex, s_rs, r_rs, s_z, r_z, s_ag, r_ag):
+def k1(hbm, gk, gc, stack, kown, cown, rk, rc, sk, sc, zk, zc, s_in, s_ex, r_ex, s_rs, r_rs, s_z, r_z, s_ag, r_ag, note):
     core = lax.axis_index("frames")
     pix = lax.axis_index("pix")
     partner = (core + 1) % 2
@@ -216,10 +226,10 @@
     load.start()
     bit = lambda t: (t % 4 + 1) // 2 % 2
     own = bit(pix) + 2 * bit(pix // 4) + 4 * bit(pix // 16)
-    mates = [((core + f) % 2, pix ^ step(e, 1)) for e in NEAR + (0,) for f in (0, 1) if e or f]
-    others = [(core, pix ^ step(e, 3)) for e in NEAR]
+    mates = [((core + f) % 2, pix ^ step(e, 1)) for e in (0,) + NEAR for f in (1, 0) if e or f]
+    across_one = [(core, pix ^ (3 * unit)) for unit in (16, 4, 1)]
     bar = pltpu.get_barrier_semaphore()
-    for device in others + mates:
+    for device in mates + across_one:
         pl.semaphore_signal(bar, inc=1, device_id=device, device_id_type=MESH)
 
     def rcopy(src, dst, ss, rs, device):
@@ -228,7 +238,7 @@
     load.wait()
     mine = stack[core]
     kown[...] = mm(mine, mine, 1, 1).reshape(8, 16, 128)
-    pl.semaphore_wait(bar, len(others + mates))
+    pl.semaphore_wait(bar, len(mates + across_one))
     ex = rcopy(stack.at[core], stack.at[core], s_ex, r_ex, (partner, pix))
     ex.start()
 
@@ -248,13 +258,21 @@
         some = buf.at[pl.ds(0, count)]
         rcopy(some, some, ss, rs, (partner, pix)).wait()
 
+    def tell(i):
+        for device in across_one:
+            pl.semaphore_signal(note.at[i], inc=1, device_id=device, device_id_type=MESH)
+
+    tell(0)
     scatter(kown, rk, 0)
     ex.wait()
     half = pl.multiple_of(core * 64, 64)
     cown[...] = mm(stack[0, pl.ds(half, 64), :], stack[1], 1, 1).reshape(8, 8, 128)
     scatter(cown, rc, 1)
+    pl.semaphore_wait(note.at[0], 3)
+    tell(1)
     wait_for(rk, s_rs.at[0], r_rs.at[0], 7)
     sk[...] = tree(rk, kown[own])
+    pl.semaphore_wait(note.at[1], 3)
     across(sk, zk, 0)
     wait_for(rc, s_rs.at[1], r_rs.at[1], 7)
     sc[...] = tree(rc, cown[own])
@@ -291,6 +309,7 @@
             pltpu.VMEM((8, 16, 128), F32),
             pltpu.VMEM((8, 8, 128), F32),
             dma(()), dma(()), dma(()), dma((2,)), dma((2,)), dma((2,)), dma((2,)), dma((2,)), dma((2,)),
+            pltpu.SemaphoreType.REGULAR((2,)),
         ],
         compiler_params=pltpu.CompilerParams(collective_id=0, has_side_effects=True, vmem_limit_bytes=32 << 20),
         name="gram_exchange",

time: 30.6 us -> 30.4 us (level)
  no operation moved by 1% of the time
where the time goes in v5:
time: 30.4 us; the launch traced here: 30.3 us
  Pallas kernels  29.6 us (97%)
  between operations  0.64 us (2%)
    pallas_call x1, Pallas kernels, call_k1(): pl.pallas_call(k1, out_shape=[jax.ShapeDtypeStruct((16, 16, 128), F32), j...  20.7 us
    pallas_call x1, Pallas kernels, call_k2(): pl.pallas_call(functools.partial(k2, core_of, opts), out_shape=[o, o], in...  8.97 us

profile of v5, /device:TPU:1, one launch (start us, length us, event | category | flops | bytes accessed | tf_op | source)
XLA Modules:
  0.0 30.3 jit_solution(17303713815252307678)
XLA Ops:
  0.6 20.7 %gram_exchange.1 = (f32[16,16,128]{2,1,0:T(8,128)S(1)}, f32[16,8,128]{2,1,0:T(8,128)S(1)}, f32[2,128,512]{2,1,0:T(8,128)S(1)}) custom-call(f32[128,512]{1,0:T(8,128)} %hbm.1), custom_call_target="tpu_custom_call" | custom-call | tf_op jit(solution)/shard_map/gram_exchange/pallas_call | solution.py:293
  21.3 9.0 %merge_project.1 = (f32[128,512]{1,0:T(8,128)}, f32[128,512]{1,0:T(8,128)}) custom-call(f32[16,16,128]{2,1,0:T(8,128)S(1)} %get-tuple-element.5.gk, f32[16,8,128]{2,1,0:T(8,128)S(1)} %get-tuple-element.6.gc, f32[2,128,512]{2,1,0:T(8,128)S(1)} %get-tuple-element.7.stack), custom_call_target="tpu_custom_call" | custom-call | tf_op jit(solution)/shard_map/merge_project/pallas_call | solution.py:202

commit v6 on v5

--- a/solution.py
+++ b/solution.py
@@ -229,7 +229,8 @@
     mates = [((core + f) % 2, pix ^ step(e, 1)) for e in (0,) + NEAR for f in (1, 0) if e or f]
     across_one = [(core, pix ^ (3 * unit)) for unit in (16, 4, 1)]
     bar = pltpu.get_barrier_semaphore()
-    for device in mates + across_one:
+    greeted = [(partner, pix)] + [(core, pix ^ step(e, 1)) for e in NEAR] + across_one
+    for device in greeted:
         pl.semaphore_signal(bar, inc=1, device_id=device, device_id_type=MESH)
 
     def rcopy(src, dst, ss, rs, device):
@@ -238,7 +239,7 @@
     load.wait()
     mine = stack[core]
     kown[...] = mm(mine, mine, 1, 1).reshape(8, 16, 128)
-    pl.semaphore_wait(bar, len(mates + across_one))
+    pl.semaphore_wait(bar, len(greeted))
     ex = rcopy(stack.at[core], stack.at[core], s_ex, r_ex, (partner, pix))
     ex.start()
 
@@ -254,9 +255,13 @@
         for device in mates:
             rcopy(g.at[core * 8 + own], g.at[core * 8 + own], s_ag.at[i], r_ag.at[i], device).start()
 
+    sent = []
+
     def wait_for(buf, ss, rs, count):
         some = buf.at[pl.ds(0, count)]
-        rcopy(some, some, ss, rs, (partner, pix)).wait()
+        copy = rcopy(some, some, ss, rs, (partner, pix))
+        copy.wait_recv()
+        sent.append(copy)
 
     def tell(i):
         for device in across_one:
@@ -285,6 +290,8 @@
     gather(gc, 1)
     wait_for(gk, s_ag.at[0], r_ag.at[0], 15)
     wait_for(gc, s_ag.at[1], r_ag.at[1], 15)
+    for copy in sent:
+        copy.wait_send()
 
 
 def call_k1(frames):

time: 30.4 us -> 30.4 us (level)
  no operation moved by 1% of the time
where the time goes in v6:
time: 30.4 us; the launch traced here: 30.3 us
  Pallas kernels  29.6 us (97%)
  between operations  0.64 us (2%)
    pallas_call x1, Pallas kernels, call_k1(): pl.pallas_call(k1, out_shape=[jax.ShapeDtypeStruct((16, 16, 128), F32), j...  20.6 us
    pallas_call x1, Pallas kernels, call_k2(): pl.pallas_call(functools.partial(k2, core_of, opts), out_shape=[o, o], in...  8.97 us

profile of v6, /device:TPU:1, one launch (start us, length us, event | category | flops | bytes accessed | tf_op | source)
XLA Modules:
  0.0 30.3 jit_solution(12306165710399271240)
XLA Ops:
  0.6 20.6 %gram_exchange.1 = (f32[16,16,128]{2,1,0:T(8,128)S(1)}, f32[16,8,128]{2,1,0:T(8,128)S(1)}, f32[2,128,512]{2,1,0:T(8,128)S(1)}) custom-call(f32[128,512]{1,0:T(8,128)} %hbm.1), custom_call_target="tpu_custom_call" | custom-call | tf_op jit(solution)/shard_map/gram_exchange/pallas_call | solution.py:300
  21.3 9.0 %merge_project.1 = (f32[128,512]{1,0:T(8,128)}, f32[128,512]{1,0:T(8,128)}) custom-call(f32[16,16,128]{2,1,0:T(8,128)S(1)} %get-tuple-element.5.gk, f32[16,8,128]{2,1,0:T(8,128)S(1)} %get-tuple-element.6.gc, f32[2,128,512]{2,1,0:T(8,128)S(1)} %get-tuple-element.7.stack), custom_call_target="tpu_custom_call" | custom-call | tf_op jit(solution)/shard_map/merge_project/pallas_call | solution.py:202

commit v7 on v6

--- a/solution.py
+++ b/solution.py
@@ -237,11 +237,11 @@
         return pltpu.make_async_remote_copy(src_ref=src, dst_ref=dst, send_sem=ss, recv_sem=rs, device_id=device, device_id_type=MESH)
 
     load.wait()
-    mine = stack[core]
-    kown[...] = mm(mine, mine, 1, 1).reshape(8, 16, 128)
     pl.semaphore_wait(bar, len(greeted))
     ex = rcopy(stack.at[core], stack.at[core], s_ex, r_ex, (partner, pix))
     ex.start()
+    mine = stack[core]
+    kown[...] = mm(mine, mine, 1, 1).reshape(8, 16, 128)
 
     def scatter(block, into, i):
         for e in NEAR:

time: 30.4 us -> 30.4 us (level)
  no operation moved by 1% of the time
where the time goes in v7:
time: 30.4 us; the launch traced here: 30.3 us
  Pallas kernels  29.6 us (97%)
  between operations  0.64 us (2%)
    pallas_call x1, Pallas kernels, call_k1(): pl.pallas_call(k1, out_shape=[jax.ShapeDtypeStruct((16, 16, 128), F32), j...  20.6 us
    pallas_call x1, Pallas kernels, call_k2(): pl.pallas_call(functools.partial(k2, core_of, opts), out_shape=[o, o], in...  8.97 us

profile of v7, /device:TPU:1, one launch (start us, length us, event | category | flops | bytes accessed | tf_op | source)
XLA Modules:
  0.0 30.3 jit_solution(15747315040978684713)
XLA Ops:
  0.6 20.6 %gram_exchange.1 = (f32[16,16,128]{2,1,0:T(8,128)S(1)}, f32[16,8,128]{2,1,0:T(8,128)S(1)}, f32[2,128,512]{2,1,0:T(8,128)S(1)}) custom-call(f32[128,512]{1,0:T(8,128)} %hbm.1), custom_call_target="tpu_custom_call" | custom-call | tf_op jit(solution)/shard_map/gram_exchange/pallas_call | solution.py:300
  21.3 9.0 %merge_project.1 = (f32[128,512]{1,0:T(8,128)}, f32[128,512]{1,0:T(8,128)}) custom-call(f32[16,16,128]{2,1,0:T(8,128)S(1)} %get-tuple-element.5.gk, f32[16,8,128]{2,1,0:T(8,128)S(1)} %get-tuple-element.6.gc, f32[2,128,512]{2,1,0:T(8,128)S(1)} %get-tuple-element.7.stack), custom_call_target="tpu_custom_call" | custom-call | tf_op jit(solution)/shard_map/merge_project/pallas_call | solution.py:202
